TPU v7x, 32 devices: a whole 2x2x4 slice. The times are simulated.
32 devices in a mesh: groups: 2 (over y), seq: 4 (over z), inner: 2 (over x), batch: 2 (over core).
Axes of the slice: x: 2, y: 2, z: 4, core: 2. Of those that a mesh axis runs over, the one named last changes fastest.
Arguments:
- queries: bfloat16 [4, 2048, 256], P(('groups', 'batch'), ('seq', 'inner')), parts along dimension 0, may hold values from -6 to 6
- keys: bfloat16 [4, 2048, 256], P(('groups', 'batch'), ('seq', 'inner')), parts along dimension 0, may hold values from -6 to 6
- values: bfloat16 [4, 2048, 256], P(('groups', 'batch'), ('seq', 'inner')), parts along dimension 0, may hold values from -6 to 6
- rates: float32 [4, 2048], P(('groups', 'batch'), ('seq', 'inner')), parts along dimension 0, may hold values from 0.05 to 1
- video_start: int32 [4], P(('groups', 'batch')), parts along dimension 0, may hold values from 0 to 511
- span_len: int32 [4, 4], P(('groups', 'batch'), 'seq'), parts along dimension 0, may hold values from 256 to 512, as said below
- init_weights: float32 [3, 256, 256], replicated, may hold values from -0.375 to 0.375
Outputs:
- outputs: bfloat16 [4, 2048, 256], P(('groups', 'batch'), ('seq', 'inner')), parts along dimension 0
- final_weights: float32 [4, 3, 256, 256], P(('groups', 'batch'), None, 'seq'), parts along dimension 0
There are 2 independent parts, one for each index of `groups`. A program takes and returns all parts, laid end to end along the dimension named above; an argument that names none is the same for every part. Nothing has to cross between parts.
Inputs may be any that keep to these rules, and one draw needn't show every extreme that they name: Every video has at least one span with span_len equal to 512.
All inputs are finite; a program needn't handle non-finite values.
Results may differ from a plain program's by a relative error of at most 0.015.
Values may be sent and summed in bfloat16 or wider, within the bound.
A program may use at most 64 MiB of HBM per device.

v0:
```python
import jax
import jax.numpy as jnp
from jax import lax
from jax.sharding import PartitionSpec as P

NS_STEPS = 5


step_size = 0.1
norm_eps = 1e-07
column_eps = 1e-06


def shifted(value, axis, steps):
    count = lax.axis_size(axis)
    initial, last = (max(0, -steps), min(count, count - steps))
    return lax.ppermute(value, axis, [(source, source + steps) for source in range(initial, last)])


def broadcast(value, axis, root):
    mine = lax.axis_index(axis) == root
    return lax.psum(jnp.where(mine, value, jnp.zeros_like(value)), axis)


def swish_parts(pre_act):
    sigma = jax.nn.sigmoid(pre_act)
    return (pre_act * sigma, sigma * (1.0 + pre_act * (1.0 - sigma)))


def apply_net(rows, half_weights):
    gate_pre = jnp.dot(rows, half_weights[0], preferred_element_type=jnp.float32)
    up_pre = jnp.dot(rows, half_weights[1], preferred_element_type=jnp.float32)
    active_part, unused_slope = swish_parts(gate_pre)
    hidden = (active_part * up_pre).astype(jnp.bfloat16)
    contract = (((1,), (1,)), ((), ()))
    return lax.dot_general(
        hidden, half_weights[2], contract, preferred_element_type=jnp.float32
    ).astype(jnp.bfloat16)


def key_grads(key_rows, value_rows, weight, half_weights):
    gate_pre = jnp.dot(key_rows, half_weights[0], preferred_element_type=jnp.float32)
    up_pre = jnp.dot(key_rows, half_weights[1], preferred_element_type=jnp.float32)
    active_part, slope_term = swish_parts(gate_pre)
    hidden = (active_part * up_pre).astype(jnp.bfloat16)
    neg_values = (-(weight[:, None] * value_rows.astype(jnp.float32))).astype(jnp.bfloat16)
    back_grad = jnp.dot(neg_values, half_weights[2], preferred_element_type=jnp.float32)
    d_upper = (back_grad * active_part).astype(jnp.bfloat16)
    d_gate = (back_grad * up_pre * slope_term).astype(jnp.bfloat16)
    contract = (((0,), (0,)), ((), ()))
    grad_one = lax.dot_general(key_rows, d_gate, contract, preferred_element_type=jnp.float32)
    grad_three = lax.dot_general(key_rows, d_upper, contract, preferred_element_type=jnp.float32)
    grad_two = lax.dot_general(neg_values, hidden, contract, preferred_element_type=jnp.float32)
    return jnp.stack([grad_one, grad_three, grad_two])


def newton(grad):
    scale = jnp.sqrt(jnp.sum(grad * grad))
    iterate = grad / (scale + norm_eps)
    for unused in range(NS_STEPS):
        gram = jnp.dot(
            iterate, iterate.T, precision=lax.Precision.HIGHEST, preferred_element_type=jnp.float32
        )
        iterate = 1.5 * iterate - 0.5 * jnp.dot(
            gram, iterate, precision=lax.Precision.HIGHEST, preferred_element_type=jnp.float32
        )
    return iterate.astype(jnp.bfloat16)


def renorm(before, moved):
    old_norm = jnp.sqrt(jnp.sum(before * before, axis=1, keepdims=True) + column_eps)
    new_norm = jnp.sqrt(jnp.sum(moved * moved, axis=1, keepdims=True) + column_eps)
    return moved * (old_norm / new_norm)


def ortho_all(total):
    return jax.vmap(newton)(total)


def ortho_none(total):
    return jnp.zeros(total.shape, jnp.bfloat16)


def pad_slots(array, slot_total):
    filler = jnp.zeros((slot_total - array.shape[0],) + tuple(array.shape[1:]), array.dtype)
    return jnp.concatenate([array, filler], axis=0)


def per_device(queries, keys, values, rates, video_start, span_len, init_weights):
    video_count, tok_rows, head_width = queries.shape
    seq_count = lax.axis_size("seq")
    inner_count = lax.axis_size("inner")
    seq_place = lax.axis_index("seq")
    inner_place = lax.axis_index("inner")
    span_rows = tok_rows * inner_count
    within = jnp.arange(tok_rows, dtype=jnp.int32) + inner_place * tok_rows
    state_shape = init_weights.shape
    per_owner = (state_shape[0] + inner_count - 1) // inner_count
    slot_total = per_owner * inner_count

    def local_terms(video_slot, state):
        half_weights = state.astype(jnp.bfloat16)
        query_rows = lax.dynamic_index_in_dim(queries, video_slot, 0, keepdims=False)
        key_rows = lax.dynamic_index_in_dim(keys, video_slot, 0, keepdims=False)
        value_rows = lax.dynamic_index_in_dim(values, video_slot, 0, keepdims=False)
        rate_rows = lax.dynamic_index_in_dim(rates, video_slot, 0, keepdims=False)
        length = lax.dynamic_index_in_dim(span_len, video_slot, 0, keepdims=False)[0]
        begin = lax.dynamic_index_in_dim(video_start, video_slot, 0, keepdims=False)
        position = seq_place * span_rows + within
        valid = ((position >= begin) & (within < length)).astype(jnp.float32)
        weight = rate_rows * valid
        partial_value = (
            key_grads(key_rows, value_rows, weight, half_weights)
            .astype(jnp.bfloat16)
            .astype(jnp.float32)
        )
        return (apply_net(query_rows, half_weights), partial_value)

    def skip_terms(video_slot, state):
        return (
            jnp.zeros((tok_rows, head_width), jnp.bfloat16),
            jnp.zeros(state_shape, jnp.float32),
        )

    final_shape = (video_count,) + tuple(state_shape)

    def step(turn_index, carry):
        incoming, outputs, finals = carry
        video_index = turn_index - seq_place
        active = (video_index >= 0) & (video_index < video_count)
        video_slot = jnp.clip(video_index, 0, video_count - 1)
        state = jnp.where(seq_place == 0, init_weights, incoming)
        out_rows, partial_value = lax.cond(active, local_terms, skip_terms, video_slot, state)
        padded = pad_slots(partial_value, slot_total)
        owned = lax.psum_scatter(
            padded.astype(jnp.bfloat16), "inner", scatter_dimension=0, tiled=True
        ).astype(jnp.float32)
        mine = lax.cond(active, ortho_all, ortho_none, owned)
        ortho = lax.all_gather(mine, "inner", axis=0, tiled=True)[: state_shape[0]]
        old_out = lax.dynamic_index_in_dim(outputs, video_slot, 0, keepdims=False)
        outputs = lax.dynamic_update_index_in_dim(
            outputs, jnp.where(active, out_rows, old_out), video_slot, 0
        )
        store = active & (seq_place == seq_count - 1)
        old_final = lax.dynamic_index_in_dim(finals, video_slot, 0, keepdims=False)
        new_state = renorm(state, state - step_size * ortho.astype(jnp.float32))
        finals = lax.dynamic_update_index_in_dim(
            finals, jnp.where(store, new_state, old_final), video_slot, 0
        )
        incoming = shifted(new_state, "seq", 1)
        return (incoming, outputs, finals)

    start_carry = (
        jnp.zeros(state_shape, jnp.float32),
        jnp.zeros(queries.shape, jnp.bfloat16),
        jnp.zeros(final_shape, jnp.float32),
    )
    last_in, outputs, finals = lax.fori_loop(0, video_count + seq_count - 1, step, start_carry)
    everything = broadcast(finals, "seq", seq_count - 1)
    row_count = head_width // seq_count
    return (outputs, lax.dynamic_slice_in_dim(everything, seq_place * row_count, row_count, 2))


def solution(mesh):
    in_specs = (
        P(("groups", "batch"), ("seq", "inner"), None),
        P(("groups", "batch"), ("seq", "inner"), None),
        P(("groups", "batch"), ("seq", "inner"), None),
        P(("groups", "batch"), ("seq", "inner")),
        P(("groups", "batch")),
        P(("groups", "batch"), "seq"),
        P(),
    )
    out_specs = (
        P(("groups", "batch"), ("seq", "inner"), None),
        P(("groups", "batch"), None, "seq", None),
    )
    return jax.shard_map(
        per_device, mesh=mesh, in_specs=in_specs, out_specs=out_specs, check_vma=False
    )
```

profile of v0, /device:TPU:26, one launch (start us, length us, event | category | flops | bytes accessed | tf_op | source)
XLA Modules:
  0.0 291.6 jit_solution(18334689422847363460)
XLA Ops:
  8.2 1.0 copy-done
  9.2 228.0 %while.19 = (s32[]{:T(128)}, f32[3,256,256]{2,1,0:T(8,128)S(1)}, bf16[1,256,256]{2,1,0:T(8,128)(2,1)S(1)}, f32[1,3,256,256]{3,2,1,0:T(8,128)S(1)}, pred[]{:T(512...) while((s32[]{:T(128)}, f32[3,256,256]{2,1,0:T(8,128)S(1)}, ...), condition=%wide.region_9.10_spmd.clone, body=%wide.region_0.9_spmd.clone.sunk | while | flops 4337240064 | bytes 41312808 | solution.py:158
  10.4 16.7 %reduce-scatter.2.cloned.1.call-done = bf16[2,256,256]{2,1,0:T(8,128)(2,1)} async-done(((bf16[4,256,256]{2,1,0:T(8,128)(2,1)}), bf16[2,256,256]{2,1,0:T(8,128)(2,1)}) %reduce-scatter.2.cloned.1.call-update) | async-done | bytes 262160 | tf_op jit(solution)/shard_map/while/body/eval_jaxpr/reduce_scatter | solution.py:135
  27.2 1.0 convert_element_type.136
  28.2 8.5 %all_gather.10 = bf16[4,256,256]{2,1,0:T(8,128)(2,1)S(1)} all-gather(bf16[2,256,256]{2,1,0:T(8,128)(2,1)S(1)} %get-tuple-element.569), channel_id=1, replica_groups=mesh['groups'=2,'seq'=4,'inner'=2,'batch'=2] {'inner'}, dimensions={0}, use_global_device_ids=true | all-gather | bytes 786432 | tf_op jit(solution)/shard_map/while/body/eval_jaxpr/all_gather | solution.py:139
  37.0 1.3 fusion.74
  38.2 1.3 collective-permute-start
  39.6 19.0 %collective-permute-done = f32[3,256,256]{2,1,0:T(8,128)S(1)} collective-permute-done((f32[3,256,256]{2,1,0:T(8,128)}, f32[3,256,256]{2,1,0:T(8,128)S(1)}, u32[]{:S(2)}, u32[]{:S(2)}) %collective-permute-start) | collective-permute-done | bytes 786464 | tf_op jit(solution)/shard_map/while/body/eval_jaxpr/ppermute | solution.py:17
  59.8 23.2 %reduce-scatter.2.cloned.1.call-done = bf16[2,256,256]{2,1,0:T(8,128)(2,1)} async-done(((bf16[4,256,256]{2,1,0:T(8,128)(2,1)}), bf16[2,256,256]{2,1,0:T(8,128)(2,1)}) %reduce-scatter.2.cloned.1.call-update) | async-done | bytes 262160 | tf_op jit(solution)/shard_map/while/body/eval_jaxpr/reduce_scatter | solution.py:135
  83.0 1.0 convert_element_type.136
  84.0 8.5 %all_gather.10 = bf16[4,256,256]{2,1,0:T(8,128)(2,1)S(1)} all-gather(bf16[2,256,256]{2,1,0:T(8,128)(2,1)S(1)} %get-tuple-element.569), channel_id=1, replica_groups=mesh['groups'=2,'seq'=4,'inner'=2,'batch'=2] {'inner'}, dimensions={0}, use_global_device_ids=true | all-gather | bytes 786432 | tf_op jit(solution)/shard_map/while/body/eval_jaxpr/all_gather | solution.py:139
  92.8 1.3 fusion.74
  94.1 1.3 collective-permute-start
  95.4 19.0 %collective-permute-done = f32[3,256,256]{2,1,0:T(8,128)S(1)} collective-permute-done((f32[3,256,256]{2,1,0:T(8,128)}, f32[3,256,256]{2,1,0:T(8,128)S(1)}, u32[]{:S(2)}, u32[]{:S(2)}) %collective-permute-start) | collective-permute-done | bytes 786464 | tf_op jit(solution)/shard_map/while/body/eval_jaxpr/ppermute | solution.py:17
  115.6 24.8 %reduce-scatter.2.cloned.1.call-done = bf16[2,256,256]{2,1,0:T(8,128)(2,1)} async-done(((bf16[4,256,256]{2,1,0:T(8,128)(2,1)}), bf16[2,256,256]{2,1,0:T(8,128)(2,1)}) %reduce-scatter.2.cloned.1.call-update) | async-done | bytes 262160 | tf_op jit(solution)/shard_map/while/body/eval_jaxpr/reduce_scatter | solution.py:135
  140.4 1.0 convert_element_type.136
  141.4 8.5 %all_gather.10 = bf16[4,256,256]{2,1,0:T(8,128)(2,1)S(1)} all-gather(bf16[2,256,256]{2,1,0:T(8,128)(2,1)S(1)} %get-tuple-element.569), channel_id=1, replica_groups=mesh['groups'=2,'seq'=4,'inner'=2,'batch'=2] {'inner'}, dimensions={0}, use_global_device_ids=true | all-gather | bytes 786432 | tf_op jit(solution)/shard_map/while/body/eval_jaxpr/all_gather | solution.py:139
  150.2 1.3 fusion.74
  151.4 1.3 collective-permute-start
  152.8 24.9 %collective-permute-done = f32[3,256,256]{2,1,0:T(8,128)S(1)} collective-permute-done((f32[3,256,256]{2,1,0:T(8,128)}, f32[3,256,256]{2,1,0:T(8,128)S(1)}, u32[]{:S(2)}, u32[]{:S(2)}) %collective-permute-start) | collective-permute-done | bytes 786464 | tf_op jit(solution)/shard_map/while/body/eval_jaxpr/ppermute | solution.py:17
  177.8 5.0 %conditional.6 = (bf16[256,256]{1,0:T(8,128)(2,1)S(1)}, bf16[3,256,256]{1,2,0:T(8,128)(2,1)S(1)}) conditional(s32[]{:T(128)} %convert_element_type.135, () %tuple.73, (bf16[1,256,256]{2,1,0:T(8,128)(2,1)}, f32[3,256,256]{2,1,0:T(8,128)S(1)}, s32[]{:T(128)}, s32[256]{0:T(256)S(1)}, s32[1]{0:T(128)}, /*index=5*/s32[1,1]{1,0:T(1,128)}, ...), branch_computations={%region_1.1_spmd, %region_2.2_spmd} | conditional | flops 305202688 | bytes 8524900 | solution.py:133
  177.9 1.3 and_select_fusion
  183.9 14.8 %reduce-scatter.2.cloned.1.call-done = bf16[2,256,256]{2,1,0:T(8,128)(2,1)} async-done(((bf16[4,256,256]{2,1,0:T(8,128)(2,1)}), bf16[2,256,256]{2,1,0:T(8,128)(2,1)}) %reduce-scatter.2.cloned.1.call-update) | async-done | bytes 262160 | tf_op jit(solution)/shard_map/while/body/eval_jaxpr/reduce_scatter | solution.py:135
  198.7 1.0 convert_element_type.136
  199.7 7.2 %conditional.7 = (bf16[2,256,256]{2,1,0:T(8,128)(2,1)S(1)}) conditional(s32[]{:T(128)} %convert_element_type.135, () %tuple.72, f32[2,256,256]{2,1,0:T(8,128)S(1)} %convert_element_type.136), branch_computations={%region_4.4_spmd, %region_5.6_spmd} | conditional | flops 4029284352 | bytes 13369392 | solution.py:138
  206.8 8.5 %all_gather.10 = bf16[4,256,256]{2,1,0:T(8,128)(2,1)S(1)} all-gather(bf16[2,256,256]{2,1,0:T(8,128)(2,1)S(1)} %get-tuple-element.569), channel_id=1, replica_groups=mesh['groups'=2,'seq'=4,'inner'=2,'batch'=2] {'inner'}, dimensions={0}, use_global_device_ids=true | all-gather | bytes 786432 | tf_op jit(solution)/shard_map/while/body/eval_jaxpr/all_gather | solution.py:139
  215.6 1.3 fusion.74
  216.9 1.3 collective-permute-start
  218.2 19.0 %collective-permute-done = f32[3,256,256]{2,1,0:T(8,128)S(1)} collective-permute-done((f32[3,256,256]{2,1,0:T(8,128)}, f32[3,256,256]{2,1,0:T(8,128)S(1)}, u32[]{:S(2)}, u32[]{:S(2)}) %collective-permute-start) | collective-permute-done | bytes 786464 | tf_op jit(solution)/shard_map/while/body/eval_jaxpr/ppermute | solution.py:17
  237.2 1.0 broadcast_select_fusion.1
  238.2 44.6 %all-reduce.3.cloned.1.call-done = f32[1,3,256,256]{3,2,1,0:T(8,128)} async-done(((f32[1,3,256,256]{3,2,1,0:T(8,128)}), f32[1,3,256,256]{3,2,1,0:T(8,128)}) %all-reduce.3.cloned.1.call-update) | async-done | bytes 786448 | tf_op jit(solution)/shard_map/psum | solution.py:22
  282.9 1.6 constant_dynamic-slice_fusion
  (97 shorter events, 16.9 us)
Async XLA Ops:
  8.0 1.1 copy-start
  8.1 1.1 copy-start.2
  8.1 1.1 copy-start.6
  9.2 18.0 %reduce-scatter.2.cloned.1.call-start = ((), (), s32[]{:S(2)}) async-start(), calls=%async_computation.2 | async-start | bytes 786432 | tf_op jit(solution)/shard_map/while/body/eval_jaxpr/reduce_scatter | solution.py:135
  36.9 21.6 %copy-start.1 = (f32[3,256,256]{2,1,0:T(8,128)S(1)}, f32[3,256,256]{2,1,0:T(8,128)}, u32[]{:S(2)}) copy-start(f32[3,256,256]{2,1,0:T(8,128)} %get-tuple-element.593) | copy-start | bytes 2359300 | tf_op jit(solution)/shard_map/while
  38.2 20.3 %collective-permute-start = (f32[3,256,256]{2,1,0:T(8,128)}, f32[3,256,256]{2,1,0:T(8,128)S(1)}, u32[]{:S(2)}, u32[]{:S(2)}) collective-permute-start(f32[3,256,256]{2,1,0:T(8,128)} %get-tuple-element.508), channel_id=1, source_target_pairs={{0,4},{4,8},{8,12},{1,5},{5,9},{9,13},{2,6},{6,10},{10,14},{3,7},{... | collective-permute-start | bytes 2359304 | tf_op jit(solution)/shard_map/while/body/eval_jaxpr/ppermute | solution.py:17
  58.6 24.4 %reduce-scatter.2.cloned.1.call-start = ((), (), s32[]{:S(2)}) async-start(), calls=%async_computation.2 | async-start | bytes 786432 | tf_op jit(solution)/shard_map/while/body/eval_jaxpr/reduce_scatter | solution.py:135
  92.8 21.6 %copy-start.1 = (f32[3,256,256]{2,1,0:T(8,128)S(1)}, f32[3,256,256]{2,1,0:T(8,128)}, u32[]{:S(2)}) copy-start(f32[3,256,256]{2,1,0:T(8,128)} %get-tuple-element.593) | copy-start | bytes 2359300 | tf_op jit(solution)/shard_map/while
  94.1 20.3 %collective-permute-start = (f32[3,256,256]{2,1,0:T(8,128)}, f32[3,256,256]{2,1,0:T(8,128)S(1)}, u32[]{:S(2)}, u32[]{:S(2)}) collective-permute-start(f32[3,256,256]{2,1,0:T(8,128)} %get-tuple-element.508), channel_id=1, source_target_pairs={{0,4},{4,8},{8,12},{1,5},{5,9},{9,13},{2,6},{6,10},{10,14},{3,7},{... | collective-permute-start | bytes 2359304 | tf_op jit(solution)/shard_map/while/body/eval_jaxpr/ppermute | solution.py:17
  114.4 26.0 %reduce-scatter.2.cloned.1.call-start = ((), (), s32[]{:S(2)}) async-start(), calls=%async_computation.2 | async-start | bytes 786432 | tf_op jit(solution)/shard_map/while/body/eval_jaxpr/reduce_scatter | solution.py:135
  150.2 27.6 %copy-start.1 = (f32[3,256,256]{2,1,0:T(8,128)S(1)}, f32[3,256,256]{2,1,0:T(8,128)}, u32[]{:S(2)}) copy-start(f32[3,256,256]{2,1,0:T(8,128)} %get-tuple-element.593) | copy-start | bytes 2359300 | tf_op jit(solution)/shard_map/while
  151.4 26.3 %collective-permute-start = (f32[3,256,256]{2,1,0:T(8,128)}, f32[3,256,256]{2,1,0:T(8,128)S(1)}, u32[]{:S(2)}, u32[]{:S(2)}) collective-permute-start(f32[3,256,256]{2,1,0:T(8,128)} %get-tuple-element.508), channel_id=1, source_target_pairs={{0,4},{4,8},{8,12},{1,5},{5,9},{9,13},{2,6},{6,10},{10,14},{3,7},{... | collective-permute-start | bytes 2359304 | tf_op jit(solution)/shard_map/while/body/eval_jaxpr/ppermute | solution.py:17
  177.7 20.9 %reduce-scatter.2.cloned.1.call-start = ((), (), s32[]{:S(2)}) async-start(), calls=%async_computation.2 | async-start | bytes 786432 | tf_op jit(solution)/shard_map/while/body/eval_jaxpr/reduce_scatter | solution.py:135
  179.2 0.9 copy-start.5
  181.4 0.9 copy-start.4
  215.6 21.6 %copy-start.1 = (f32[3,256,256]{2,1,0:T(8,128)S(1)}, f32[3,256,256]{2,1,0:T(8,128)}, u32[]{:S(2)}) copy-start(f32[3,256,256]{2,1,0:T(8,128)} %get-tuple-element.593) | copy-start | bytes 2359300 | tf_op jit(solution)/shard_map/while
  216.9 20.3 %collective-permute-start = (f32[3,256,256]{2,1,0:T(8,128)}, f32[3,256,256]{2,1,0:T(8,128)S(1)}, u32[]{:S(2)}, u32[]{:S(2)}) collective-permute-start(f32[3,256,256]{2,1,0:T(8,128)} %get-tuple-element.508), channel_id=1, source_target_pairs={{0,4},{4,8},{8,12},{1,5},{5,9},{9,13},{2,6},{6,10},{10,14},{3,7},{... | collective-permute-start | bytes 2359304 | tf_op jit(solution)/shard_map/while/body/eval_jaxpr/ppermute | solution.py:17
  237.2 1.0 copy-start.3
  237.2 45.6 %all-reduce.3.cloned.1.call-start = ((), (), s32[]{:S(2)}) async-start(), calls=%async_computation.1 | async-start | bytes 1572864 | tf_op jit(solution)/shard_map/psum | solution.py:22
Sparse Core Ops, SparseCore 0:
  12.2 14.8 reduce-scatter.1
  61.6 21.3 reduce-scatter.1
  117.4 22.8 reduce-scatter.1
  184.0 14.6 reduce-scatter.1
Sparse Core Ops, SparseCore 1:
  240.0 42.8 all-reduce.2
where the time goes:
time: 296 us; the launch traced here: 292 us
  waiting for transfers between devices  206 us (70%)
  blocking collectives  34.2 us (12%)
  between operations  15.2 us (5%)
  other arithmetic  12.9 us (4%)
  matrix products  8.87 us (3%)
  local copies, waits for them, and re-layouts  8.5 us (3%)
  starting transfers between devices  5.13 us (2%)
    ppermute x4, waiting for transfers between devices, shifted(): lax.ppermute(value, axis, [(source, source + steps) for source in range(i...  82 us
    reduce_scatter x4, waiting for transfers between devices, step(): lax.psum_scatter(padded.astype(jnp.bfloat16), 'inner', scatter_dimension=...  79.5 us
    psum x1, waiting for transfers between devices, broadcast(): return lax.psum(jnp.where(mine, value, jnp.zeros_like(value)), axis)  44.6 us
    all_gather x4, blocking collectives, step(): ortho = lax.all_gather(mine, 'inner', axis=0, tiled=True)[:state_shape[0]]  34.2 us
  transfers between devices with their start and end apart: 9, of which 9 were waited for; matrix products, arithmetic and copies ran while one was open for 0% of the time, Pallas kernels for 0%

commit v1 on v0

v1 whole, which is shorter than its diff:
```python
import functools

import jax
import jax.numpy as jnp
from jax import lax
from jax.experimental import pallas as pl
from jax.experimental.pallas import tpu as pltpu
from jax.sharding import PartitionSpec as P

NS_STEPS = 5
step_size = 0.1
norm_eps = 1e-07
column_eps = 1e-06
F32, BF16 = jnp.float32, jnp.bfloat16


def dot(a, b, ca, cb):
    return lax.dot_general(a, b, (((ca,), (cb,)), ((), ())), preferred_element_type=F32)


def apply_net(rows, w1, w3, w2):
    gate = dot(rows, w1, 1, 0)
    up = dot(rows, w3, 1, 0)
    hidden = (gate * jax.nn.sigmoid(gate) * up).astype(BF16)
    return dot(hidden, w2, 1, 1).astype(BF16)


def span_grads(k, nv, w1, w3, w2):
    gate = dot(k, w1, 1, 0)
    up = dot(k, w3, 1, 0)
    back = dot(nv, w2, 1, 0)
    s = jax.nn.sigmoid(gate)
    active = gate * s
    hidden = (active * up).astype(BF16)
    d_up = (back * active).astype(BF16)
    d_gate = (back * up * (s * (1.0 + gate * (1.0 - s)))).astype(BF16)
    return [dot(k, d_gate, 0, 0), dot(k, d_up, 0, 0), dot(nv, hidden, 0, 0)]


def newton(grads):
    xs = [g * (1.0 / (jnp.sqrt(jnp.sum(g * g, keepdims=True)) + norm_eps)) for g in grads]
    for unused in range(NS_STEPS):
        halves = [x.astype(BF16) for x in xs]
        grams = [dot(h, h, 1, 1).astype(BF16) for h in halves]
        xs = [1.5 * x - 0.5 * dot(g, h, 1, 0) for x, g, h in zip(xs, grams, halves)]
    return xs


def chain_step(c, me, kv_ref, q_ref, state_ref, norm_ref, out_ref):
    inner, pair, tok, head = kv_ref.shape[1:]
    w1, w3, w2 = [state_ref[i].astype(BF16) for i in range(3)]

    @pl.when(c == me)
    def _():
        out_ref[...] = apply_net(q_ref[...], w1, w3, w2)

    k = kv_ref[c, :, 0].reshape(inner * tok, head)
    nv = kv_ref[c, :, 1].reshape(inner * tok, head)
    xs = newton(span_grads(k, nv, w1, w3, w2))
    for i in range(3):
        moved = state_ref[i] - step_size * xs[i].astype(BF16).astype(F32)
        before = norm_ref[i]
        after = jnp.sum(moved * moved, axis=0, keepdims=True)
        ratio = (before + column_eps) / (after + column_eps)
        state_ref[i] = moved * jnp.sqrt(ratio)
        norm_ref[i] = after * ratio


def kernel(kv_ref, q_ref, init_ref, out_ref, final_ref, state_ref, norm_ref):
    seq_count = kv_ref.shape[0]
    me = lax.axis_index("seq")
    for i in range(3):
        w = init_ref[i]
        state_ref[i] = w
        norm_ref[i] = jnp.sum(w * w, axis=0, keepdims=True)

    @pl.loop(0, seq_count)
    def _(c):
        chain_step(c, me, kv_ref, q_ref, state_ref, norm_ref, out_ref)

    rows = final_ref.shape[1]
    final_ref[...] = state_ref[:, pl.ds(pl.multiple_of(me * rows, rows), rows), :]


def per_device(queries, keys, values, rates, video_start, span_len, init_weights):
    tok, head = queries.shape[1:]
    seq_count = lax.axis_size("seq")
    inner_count = lax.axis_size("inner")
    within = jnp.arange(tok, dtype=jnp.int32) + lax.axis_index("inner") * tok
    position = lax.axis_index("seq") * tok * inner_count + within
    valid = ((position >= video_start[0]) & (within < span_len[0, 0])).astype(F32)
    weight = rates[0] * valid
    nv = (-(weight[:, None] * values[0].astype(F32))).astype(BF16)
    kv = jnp.stack([keys[0], nv])
    kv = lax.all_gather(kv, ("seq", "inner"), axis=0, tiled=False)
    kv = kv.reshape(seq_count, inner_count, 2, tok, head)
    rows = init_weights.shape[1] // seq_count
    vm = pl.BlockSpec(memory_space=pltpu.VMEM)
    out, final = pl.pallas_call(
        kernel,
        out_shape=(
            jax.ShapeDtypeStruct((tok, head), BF16),
            jax.ShapeDtypeStruct((3, rows, init_weights.shape[2]), F32),
        ),
        in_specs=[vm] * 3,
        out_specs=(vm, vm),
        scratch_shapes=[
            pltpu.VMEM(init_weights.shape, F32),
            pltpu.VMEM((3, 1, init_weights.shape[2]), F32),
        ],
    )(kv, queries[0], init_weights)
    return out[None], final[None]


def solution(mesh):
    in_specs = (
        P(("groups", "batch"), ("seq", "inner"), None),
        P(("groups", "batch"), ("seq", "inner"), None),
        P(("groups", "batch"), ("seq", "inner"), None),
        P(("groups", "batch"), ("seq", "inner")),
        P(("groups", "batch")),
        P(("groups", "batch"), "seq"),
        P(),
    )
    out_specs = (
        P(("groups", "batch"), ("seq", "inner"), None),
        P(("groups", "batch"), None, "seq", None),
    )
    return jax.shard_map(
        per_device, mesh=mesh, in_specs=in_specs, out_specs=out_specs, check_vma=False
    )
```

time: 296 us -> 85.3 us (0.29)
  the two profiles are of different devices: /device:TPU:26 before, /device:TPU:0 now
where the time goes in v1:
time: 85.3 us; the launch traced here: 85 us
  waiting for transfers between devices  52 us (61%)
  between operations  15.3 us (18%)
  Pallas kernels  14.4 us (17%)
  other arithmetic  3.34 us (4%)
    all_gather x1, waiting for transfers between devices, per_device(): kv = lax.all_gather(kv, ('seq', 'inner'), axis=0, tiled=False)  52 us
    pallas_call x1, Pallas kernels, per_device(): pl.pallas_call(kernel, out_shape=(jax.ShapeDtypeStruct((tok, head), BF16)...  14.4 us
  transfers between devices with their start and end apart: 1, of which 1 were waited for; matrix products, arithmetic and copies ran while one was open for 0% of the time, Pallas kernels for 0%

profile of v1, /device:TPU:0, one launch (start us, length us, event | category | flops | bytes accessed | tf_op | source)
XLA Modules:
  0.0 85.0 jit_solution(1585170746985015597)
XLA Ops:
  7.2 0.0 all-gather.3.cloned.1.call-start
  8.5 0.7 and_select_fusion
  9.2 1.0 %negate_convert_fusion = bf16[1,256,256]{2,1,0:T(8,128)(2,1)S(1)} fusion(bf16[1,256,256]{2,1,0:T(8,128)(2,1)} %param.9, f32[256]{0:T(256)S(1)} %and_select_fusion), kind=kLoop, calls=%fused_computation.1 | loop fusion | flops 262144 | bytes 263168 | tf_op jit(solution)/shard_map/convert_element_type | solution.py:93
  10.2 1.7 %pad_maximum_fusion = bf16[2,256,256]{2,1,0:T(8,128)(2,1)} fusion(bf16[1,256,256]{2,1,0:T(8,128)(2,1)S(1)} %negate_convert_fusion, bf16[1,256,256]{2,1,0:T(8,128)(2,1)} %param.8), kind=kLoop, calls=%fused_computation | loop fusion | flops 131072 | bytes 524288 | tf_op jit(solution)/shard_map/stack | solution.py:94
  11.9 0.0 all-gather.3.cloned.1.call-update
  11.9 52.0 %all-gather.3.cloned.1.call-done = bf16[16,256,256]{2,1,0:T(8,128)(2,1)} async-done(((bf16[2,256,256]{2,1,0:T(8,128)(2,1)}), bf16[16,256,256]{2,1,0:T(8,128)(2,1)}) %all-gather.3.cloned.1.call-update) | async-done | bytes 2097168 | tf_op jit(solution)/shard_map/all_gather | solution.py:95
  63.8 14.4 %shard_map.86 = (bf16[256,256]{1,0:T(8,128)(2,1)}, f32[3,64,256]{2,1,0:T(8,128)}) custom-call(bf16[4,2,2,256,256]{4,3,2,1,0:T(8,128)(2,1)} %bitcast.9, bf16[256,256]{1,0:T(8,128)(2,1)} %bitcast.10, f32[3,256,256]{2,1,0:T(8,128)} %init_ref.1), custom_call_target="tpu_custom_call" | custom-call | tf_op jit(solution)/shard_map/pallas_call | solution.py:99
Async XLA Ops:
  7.2 56.7 %all-gather.3.cloned.1.call-start = ((), (), s32[]{:S(2)}) async-start(), calls=%async_computation | async-start | bytes 2359296 | tf_op jit(solution)/shard_map/all_gather | solution.py:95
Sparse Core Ops, SparseCore 0:
  12.0 51.7 all-gather.2

commit v2 on v1

v2 whole, which is shorter than its diff:
```python
import functools

import jax
import jax.numpy as jnp
from jax import lax
from jax.experimental import pallas as pl
from jax.experimental.pallas import tpu as pltpu
from jax.sharding import PartitionSpec as P

NS_STEPS = 5
CHUNKS = 4
MESH = pl.DeviceIdType.MESH
step_size = 0.1
norm_eps = 1e-07
column_eps = 1e-06
F32, BF16 = jnp.float32, jnp.bfloat16


def dot(a, b, ca, cb):
    return lax.dot_general(a, b, (((ca,), (cb,)), ((), ())), preferred_element_type=F32)


def apply_net(rows, w1, w3, w2):
    gate = dot(rows, w1, 1, 0)
    up = dot(rows, w3, 1, 0)
    hidden = (gate * jax.nn.sigmoid(gate) * up).astype(BF16)
    return dot(hidden, w2, 1, 1).astype(BF16)


def span_grads(k, nv, w1, w3, w2):
    gate = dot(k, w1, 1, 0)
    up = dot(k, w3, 1, 0)
    back = dot(nv, w2, 1, 0)
    s = jax.nn.sigmoid(gate)
    active = gate * s
    hidden = (active * up).astype(BF16)
    d_up = (back * active).astype(BF16)
    d_gate = (back * up * (s * (1.0 + gate * (1.0 - s)))).astype(BF16)
    return [dot(k, d_gate, 0, 0), dot(k, d_up, 0, 0), dot(nv, hidden, 0, 0)]


def newton(grads):
    xs = [g * (1.0 / (jnp.sqrt(jnp.sum(g * g, keepdims=True)) + norm_eps)) for g in grads]
    for unused in range(NS_STEPS):
        halves = [x.astype(BF16) for x in xs]
        grams = [dot(h, h, 1, 1).astype(BF16) for h in halves]
        xs = [1.5 * x - 0.5 * dot(g, h, 1, 0) for x, g, h in zip(xs, grams, halves)]
    return xs


def kernel(
    n, m, start_ref, len_ref, key_ref, value_ref, rate_ref, q_ref, init_ref, out_ref, final_ref,
    kv, state, norm, grad, z_recv, up_send, down_send, x_recv, x_send,
):
    z, x = lax.axis_index("seq"), lax.axis_index("inner")
    tok = key_ref.shape[0]
    chunks, pair, part, head = kv.shape[2:]

    barrier = pltpu.get_barrier_semaphore()

    def greet(where):
        pl.semaphore_signal(barrier, inc=1, device_id=where, device_id_type=MESH)

    pl.when(z > 0)(lambda: greet({"seq": z - 1}))
    pl.when(z < n - 1)(lambda: greet({"seq": z + 1}))
    for r in range(1, m):
        greet({"inner": lax.rem(x + r, m)})

    within = lax.broadcasted_iota(jnp.int32, (1, tok), 1) + x * tok
    position = within + z * (tok * m)
    valid = ((position >= start_ref[0]) & (within < len_ref[0, 0])).astype(F32)
    weight = rate_ref[...] * valid
    eye = lax.broadcasted_iota(jnp.int32, (tok, tok), 0) == lax.broadcasted_iota(
        jnp.int32, (tok, tok), 1
    )
    column = jnp.sum(jnp.where(eye, weight, 0.0), axis=1, keepdims=True)
    neg = (-(column * value_ref[...].astype(F32))).astype(BF16)
    for j in range(chunks):
        kv[z, x, j, 0] = key_ref[j * part : (j + 1) * part, :]
        kv[z, x, j, 1] = neg[j * part : (j + 1) * part, :]
    for i in range(3):
        w = init_ref[i]
        state[i] = w
        norm[i] = jnp.sum(w * w, axis=0, keepdims=True)

    pl.semaphore_wait(barrier, (m - 1) + (z > 0).astype(jnp.int32) + (z < n - 1).astype(jnp.int32))

    def up(c, j):
        block = kv.at[c, x, j]
        return pltpu.make_async_remote_copy(
            block, block, up_send.at[c, j], z_recv.at[c, j], {"seq": z + 1}, MESH
        )

    def down(c, j):
        block = kv.at[c, x, j]
        return pltpu.make_async_remote_copy(
            block, block, down_send.at[c, j], z_recv.at[c, j], {"seq": z - 1}, MESH
        )

    def across(c, j, r):
        block = kv.at[c, x, j]
        return pltpu.make_async_remote_copy(
            block, block, x_send.at[r - 1, c, j], x_recv.at[r - 1, c, j],
            {"inner": lax.rem(x + r, m)}, MESH,
        )

    def send_across(c, j):
        for r in range(1, m):
            across(c, j, r).start()

    for j in range(chunks):
        early = (z < n - 1) & ((z == 0) | (j < 2 * z))
        pl.when(early)(lambda: up(z, j).start())
        pl.when(z > 0)(lambda: down(z, j).start())
        send_across(z, j)

    def phase(p):
        @pl.when(p < z)
        def _():
            for j in range(chunks):
                up(p, j).wait_recv()
                pl.when(z < n - 1)(lambda: up(p, j).start())
                send_across(p, j)

        @pl.when(p == z - 1)
        def _():
            for j in range(chunks):
                late = (z < n - 1) & (j >= 2 * z)
                pl.when(late)(lambda: up(z, j).start())

            @pl.loop(z + 1, jnp.minimum(z + 1 + p, n))
            def _(c):
                for j in range(chunks):
                    send_across(c, j)

        d = z + 1 + p

        @pl.when(d < n)
        def _():
            for j in range(chunks):
                down(d, j).wait_recv()
                pl.when(z > 0)(lambda: down(d, j).start())
                pl.when(p >= z - 1)(lambda: send_across(d, j))

    phase(0)

    @pl.loop(0, n)
    def _(c):
        for j in range(chunks):
            for r in range(1, m):
                across(c, j, r).wait_recv()
        w1, w3, w2 = [state[i].astype(BF16) for i in range(3)]

        @pl.when(c == z)
        def _():
            out_ref[...] = apply_net(q_ref[...], w1, w3, w2)

        k = kv[c, :, :, 0].reshape(m * tok, head)
        nv = kv[c, :, :, 1].reshape(m * tok, head)
        for i, g in enumerate(span_grads(k, nv, w1, w3, w2)):
            grad[i] = g
        phase(c + 1)
        xs = newton([grad[i] for i in range(3)])
        for i in range(3):
            moved = state[i] - step_size * xs[i].astype(BF16).astype(F32)
            after = jnp.sum(moved * moved, axis=0, keepdims=True)
            ratio = (norm[i] + column_eps) / (after + column_eps)
            state[i] = moved * jnp.sqrt(ratio)
            norm[i] = after * ratio

    rows = final_ref.shape[1]
    final_ref[...] = state[:, pl.ds(pl.multiple_of(z * rows, rows), rows), :]

    @pl.loop(0, n)
    def _(c):
        for j in range(chunks):
            pl.when((c <= z) & (z < n - 1))(lambda: up(c, j).wait_send())
            pl.when((c >= z) & (z > 0))(lambda: down(c, j).wait_send())
            for r in range(1, m):
                across(c, j, r).wait_send()


def per_device(queries, keys, values, rates, video_start, span_len, init_weights):
    tok, head = queries.shape[1:]
    n, m = lax.axis_size("seq"), lax.axis_size("inner")
    rows = init_weights.shape[1] // n
    vm = pl.BlockSpec(memory_space=pltpu.VMEM)
    sm = pl.BlockSpec(memory_space=pltpu.SMEM)
    dma = pltpu.SemaphoreType.DMA
    out, final = pl.pallas_call(
        functools.partial(kernel, n, m),
        out_shape=(
            jax.ShapeDtypeStruct((tok, head), BF16),
            jax.ShapeDtypeStruct((3, rows, init_weights.shape[2]), F32),
        ),
        in_specs=[sm, sm, vm, vm, vm, vm, vm],
        out_specs=(vm, vm),
        scratch_shapes=[
            pltpu.VMEM((n, m, CHUNKS, 2, tok // CHUNKS, head), BF16),
            pltpu.VMEM(init_weights.shape, F32),
            pltpu.VMEM((3, 1, init_weights.shape[2]), F32),
            pltpu.VMEM(init_weights.shape, F32),
            dma((n, CHUNKS)),
            dma((n, CHUNKS)),
            dma((n, CHUNKS)),
            dma((m - 1, n, CHUNKS)),
            dma((m - 1, n, CHUNKS)),
        ],
        compiler_params=pltpu.CompilerParams(collective_id=0, has_side_effects=True),
    )(video_start, span_len, keys[0], values[0], rates, queries[0], init_weights)
    return out[None], final[None]


def solution(mesh):
    in_specs = (
        P(("groups", "batch"), ("seq", "inner"), None),
        P(("groups", "batch"), ("seq", "inner"), None),
        P(("groups", "batch"), ("seq", "inner"), None),
        P(("groups", "batch"), ("seq", "inner")),
        P(("groups", "batch")),
        P(("groups", "batch"), "seq"),
        P(),
    )
    out_specs = (
        P(("groups", "batch"), ("seq", "inner"), None),
        P(("groups", "batch"), None, "seq", None),
    )
    return jax.shard_map(
        per_device, mesh=mesh, in_specs=in_specs, out_specs=out_specs, check_vma=False
    )
```

time: 85.3 us -> 48.6 us (0.57)
  the two profiles are of different devices: /device:TPU:0 before, /device:TPU:24 now
where the time goes in v2:
time: 48.6 us; the launch traced here: 48.4 us
  Pallas kernels  44.2 us (91%)
  local copies, waits for them, and re-layouts  2.29 us (5%)
  between operations  1.94 us (4%)
    pallas_call x1, Pallas kernels, per_device(): pl.pallas_call(functools.partial(kernel, n, m), out_shape=(jax.ShapeDtype...  44.2 us
    unnamed x4, local copies, waits for them, and re-layouts  2.29 us

profile of v2, /device:TPU:24, one launch (start us, length us, event | category | flops | bytes accessed | tf_op | source)
XLA Modules:
  0.0 48.4 jit_solution(17126050040755026939)
XLA Ops:
  1.9 44.2 %shard_map.86 = (bf16[256,256]{1,0:T(8,128)(2,1)}, f32[3,64,256]{2,1,0:T(8,128)}) custom-call(s32[1]{0:T(128)S(6)} %copy.11.start_ref, s32[1,1]{1,0:T(1,128)S(6)} %copy.12.len_ref, bf16[256,256]{1,0:T(8,128)(2,1)} %bitcast.6, bf16[256,256]{1,0:T(8,128)(2,1)} %bitcast.7, f32[1,256]{1,0:T(1,128)} %rate_ref.1, bf16[256,256]{1,0:T(8,128)(2,1)} %bitcast.8, ...), custom_call_target="tpu_custom_call" | custom-call | tf_op jit(solution)/shard_map/pallas_call | solution.py:190
  46.1 0.0 copy-start
  46.1 1.6 %copy.13 = bf16[1,256,256]{2,1,0:T(8,128)(2,1)} copy(bf16[1,256,256]{2,1,0:T(8,128)(2,1)} %bitcast.9) | data formatting | bytes 262144
  47.7 0.0 copy-done
  47.7 0.7 %copy.14 = f32[1,3,64,256]{3,2,1,0:T(8,128)} copy(f32[1,3,64,256]{3,2,1,0:T(8,128)S(1)} %bitcast.5) | data formatting | bytes 393216
Async XLA Ops:
  46.1 1.6 %copy-start = (f32[3,64,256]{2,1,0:T(8,128)S(1)}, f32[3,64,256]{2,1,0:T(8,128)}, u32[]{:S(2)}) copy-start(f32[3,64,256]{2,1,0:T(8,128)} %get-tuple-element.5) | copy-start | bytes 589828

commit v3 on v1

v3 whole, which is shorter than its diff:
```python
import functools

import jax
import jax.numpy as jnp
from jax import lax
from jax.experimental import pallas as pl
from jax.experimental.pallas import tpu as pltpu
from jax.sharding import PartitionSpec as P

NS_STEPS = 5
CHUNKS = 4
MESH = pl.DeviceIdType.MESH
step_size = 0.1
norm_eps = 1e-07
column_eps = 1e-06
F32, BF16 = jnp.float32, jnp.bfloat16


def dot(a, b, ca, cb):
    return lax.dot_general(a, b, (((ca,), (cb,)), ((), ())), preferred_element_type=F32)


def apply_net(rows, w1, w3, w2):
    gate = dot(rows, w1, 1, 0)
    up = dot(rows, w3, 1, 0)
    hidden = (gate * jax.nn.sigmoid(gate) * up).astype(BF16)
    return dot(hidden, w2, 1, 1).astype(BF16)


def span_grads(k, nv, w1, w3, w2):
    gate = dot(k, w1, 1, 0)
    up = dot(k, w3, 1, 0)
    back = dot(nv, w2, 1, 0)
    s = jax.nn.sigmoid(gate)
    active = gate * s
    hidden = (active * up).astype(BF16)
    d_up = (back * active).astype(BF16)
    d_gate = (back * up * (s * (1.0 + gate * (1.0 - s)))).astype(BF16)
    return [dot(k, d_gate, 0, 0), dot(k, d_up, 0, 0), dot(nv, hidden, 0, 0)]


def newton(grads):
    xs = [g * (1.0 / (jnp.sqrt(jnp.sum(g * g, keepdims=True)) + norm_eps)) for g in grads]
    for unused in range(NS_STEPS):
        halves = [x.astype(BF16) for x in xs]
        grams = [dot(h, h, 1, 1).astype(BF16) for h in halves]
        xs = [1.5 * x - 0.5 * dot(g, h, 1, 0) for x, g, h in zip(xs, grams, halves)]
    return xs


def kernel(
    n, m, start_ref, len_ref, key_ref, value_ref, rate_ref, q_ref, init_ref, out_ref, final_ref,
    kv, queue, outs, state, norm, grad,
    give_send, give_recv, q_send, q_recv, o_send, o_recv, f_send, f_recv, z_recv, up_send, down_send,
):
    z, x = lax.axis_index("seq"), lax.axis_index("inner")
    chief = lax.rem(lax.axis_index("batch"), m)
    place = lax.rem(x - chief + m, m)
    active = place == 0
    tok = key_ref.shape[0]
    chunks, pair, part, head = kv.shape[2:]
    rows = final_ref.shape[1]
    mine = pl.ds(pl.multiple_of(z * rows, rows), rows)

    barrier = pltpu.get_barrier_semaphore()

    def greet(where):
        pl.semaphore_signal(barrier, inc=1, device_id=where, device_id_type=MESH)

    def helper(r):
        return {"inner": lax.rem(chief + r, m)}

    @pl.when(active)
    def _():
        pl.when(z > 0)(lambda: greet({"seq": z - 1}))
        pl.when(z < n - 1)(lambda: greet({"seq": z + 1}))
        for r in range(1, m):
            greet(helper(r))

    @pl.when(jnp.logical_not(active))
    def _():
        greet({"inner": chief})

    within = lax.broadcasted_iota(jnp.int32, (1, tok), 1) + x * tok
    position = within + z * (tok * m)
    valid = ((position >= start_ref[0]) & (within < len_ref[0, 0])).astype(F32)
    weight = rate_ref[...] * valid
    eye = lax.broadcasted_iota(jnp.int32, (tok, tok), 0) == lax.broadcasted_iota(
        jnp.int32, (tok, tok), 1
    )
    column = jnp.sum(jnp.where(eye, weight, 0.0), axis=1, keepdims=True)
    neg = (-(column * value_ref[...].astype(F32))).astype(BF16)
    for j in range(chunks):
        kv[z, place, j, 0] = key_ref[j * part : (j + 1) * part, :]
        kv[z, place, j, 1] = neg[j * part : (j + 1) * part, :]

    def copy(src, dst, send, recv, where):
        return pltpu.make_async_remote_copy(src, dst, send, recv, where, MESH)

    def give(r, j):
        block = kv.at[z, r, j]
        return copy(block, block, give_send.at[j], give_recv.at[r, j], {"inner": chief})

    def give_q(r):
        return copy(q_ref, queue.at[r], q_send.at[0], q_recv.at[r], {"inner": chief})

    def give_out(r):
        return copy(outs.at[r], out_ref, o_send.at[r], o_recv.at[0], helper(r))

    def give_final(r, i):
        return copy(state.at[i, mine], final_ref.at[i], f_send.at[r, i], f_recv.at[i], helper(r))

    def up(c, r, j):
        block = kv.at[c, r, j]
        return copy(block, block, up_send.at[c, r, j], z_recv.at[c, r, j], {"seq": z + 1})

    def down(c, r, j):
        block = kv.at[c, r, j]
        return copy(block, block, down_send.at[c, r, j], z_recv.at[c, r, j], {"seq": z - 1})

    @pl.when(jnp.logical_not(active))
    def _():
        pl.semaphore_wait(barrier, 1)
        for j in range(chunks):
            give(place, j).start()
        give_q(place).start()
        for j in range(chunks):
            give(place, j).wait_send()
        give_q(place).wait_send()
        give_out(0).wait_recv()
        for i in range(3):
            give_final(0, i).wait_recv()

    def relay_up(c, first, last):
        for r in range(first, last):
            for j in range(chunks):
                up(c, r, j).wait_recv()
                pl.when(z < n - 1)(lambda: up(c, r, j).start())

    def phase(p, first):
        pl.when(p < z)(lambda: relay_up(p, first, m))

        @pl.when((p == z - 1) & (z < n - 1))
        def _():
            for r in range(1, m):
                for j in range(chunks):
                    up(z, r, j).start()

        d = z + 1 + p - (z == 0).astype(jnp.int32)

        @pl.when((d < n) & (d > z))
        def _():
            for r in range(m):
                for j in range(chunks):
                    down(d, r, j).wait_recv()
                    pl.when(z > 0)(lambda: down(d, r, j).start())

    @pl.when(active)
    def _():
        for i in range(3):
            w = init_ref[i]
            state[i] = w
            norm[i] = jnp.sum(w * w, axis=0, keepdims=True)
        pl.semaphore_wait(
            barrier, (m - 1) + (z > 0).astype(jnp.int32) + (z < n - 1).astype(jnp.int32)
        )
        for j in range(chunks):
            pl.when(z < n - 1)(lambda: up(z, 0, j).start())
            pl.when(z > 0)(lambda: down(z, 0, j).start())
        pl.when(z > 0)(lambda: relay_up(0, 0, 1))
        for r in range(1, m):
            for j in range(chunks):
                give(r, j).wait_recv()
                pl.when(z == 0)(lambda: up(z, r, j).start())
                pl.when(z > 0)(lambda: down(z, r, j).start())
        phase(0, 1)
        for r in range(1, m):
            give_q(r).wait_recv()

        @pl.loop(0, n)
        def _(c):
            w1, w3, w2 = [state[i].astype(BF16) for i in range(3)]

            @pl.when(c == z)
            def _():
                for r in range(1, m):
                    outs[r] = apply_net(queue[r], w1, w3, w2)
                out_ref[...] = apply_net(q_ref[...], w1, w3, w2)

            k = kv[c, :, :, 0].reshape(m * tok, head)
            nv = kv[c, :, :, 1].reshape(m * tok, head)
            for i, g in enumerate(span_grads(k, nv, w1, w3, w2)):
                grad[i] = g

            @pl.when(c == z)
            def _():
                for r in range(1, m):
                    give_out(r).start()

            phase(c + 1, 0)
            xs = newton([grad[i] for i in range(3)])
            for i in range(3):
                moved = state[i] - step_size * xs[i].astype(BF16).astype(F32)
                after = jnp.sum(moved * moved, axis=0, keepdims=True)
                ratio = (norm[i] + column_eps) / (after + column_eps)
                state[i] = moved * jnp.sqrt(ratio)
                norm[i] = after * ratio

        final_ref[...] = state[:, mine, :]
        for i in range(3):
            for r in range(1, m):
                give_final(r, i).start()

        @pl.loop(0, n)
        def _(c):
            for r in range(m):
                for j in range(chunks):
                    pl.when((c <= z) & (z < n - 1))(lambda: up(c, r, j).wait_send())
                    pl.when((c >= z) & (z > 0))(lambda: down(c, r, j).wait_send())

        for r in range(1, m):
            give_out(r).wait_send()
            for i in range(3):
                give_final(r, i).wait_send()


def per_device(queries, keys, values, rates, video_start, span_len, init_weights):
    tok, head = queries.shape[1:]
    n, m = lax.axis_size("seq"), lax.axis_size("inner")
    hidden = init_weights.shape[2]
    rows = init_weights.shape[1] // n
    vm = pl.BlockSpec(memory_space=pltpu.VMEM)
    sm = pl.BlockSpec(memory_space=pltpu.SMEM)
    dma = pltpu.SemaphoreType.DMA
    out, final = pl.pallas_call(
        functools.partial(kernel, n, m),
        out_shape=(
            jax.ShapeDtypeStruct((tok, head), BF16),
            jax.ShapeDtypeStruct((3, rows, hidden), F32),
        ),
        in_specs=[sm, sm, vm, vm, vm, vm, vm],
        out_specs=(vm, vm),
        scratch_shapes=[
            pltpu.VMEM((n, m, CHUNKS, 2, tok // CHUNKS, head), BF16),
            pltpu.VMEM((m, tok, head), BF16),
            pltpu.VMEM((m, tok, head), BF16),
            pltpu.VMEM(init_weights.shape, F32),
            pltpu.VMEM((3, 1, hidden), F32),
            pltpu.VMEM(init_weights.shape, F32),
            dma((CHUNKS,)),
            dma((m, CHUNKS)),
            dma((1,)),
            dma((m,)),
            dma((m,)),
            dma((1,)),
            dma((m, 3)),
            dma((3,)),
            dma((n, m, CHUNKS)),
            dma((n, m, CHUNKS)),
            dma((n, m, CHUNKS)),
        ],
        compiler_params=pltpu.CompilerParams(collective_id=0, has_side_effects=True),
    )(video_start, span_len, keys[0], values[0], rates, queries[0], init_weights)
    return out[None], final[None]


def solution(mesh):
    in_specs = (
        P(("groups", "batch"), ("seq", "inner"), None),
        P(("groups", "batch"), ("seq", "inner"), None),
        P(("groups", "batch"), ("seq", "inner"), None),
        P(("groups", "batch"), ("seq", "inner")),
        P(("groups", "batch")),
        P(("groups", "batch"), "seq"),
        P(),
    )
    out_specs = (
        P(("groups", "batch"), ("seq", "inner"), None),
        P(("groups", "batch"), None, "seq", None),
    )
    return jax.shard_map(
        per_device, mesh=mesh, in_specs=in_specs, out_specs=out_specs, check_vma=False
    )
```

time: 85.3 us -> 49.8 us (0.58)
  the two profiles are of different devices: /device:TPU:0 before, /device:TPU:26 now
where the time goes in v3:
time: 49.8 us; the launch traced here: 49.6 us
  Pallas kernels  45.4 us (91%)
  local copies, waits for them, and re-layouts  2.29 us (5%)
  between operations  1.94 us (4%)
    pallas_call x1, Pallas kernels, per_device(): pl.pallas_call(functools.partial(kernel, n, m), out_shape=(jax.ShapeDtype...  45.4 us
    unnamed x4, local copies, waits for them, and re-layouts  2.29 us

profile of v3, /device:TPU:26, one launch (start us, length us, event | category | flops | bytes accessed | tf_op | source)
XLA Modules:
  0.0 49.6 jit_solution(9337344899681148997)
XLA Ops:
  1.9 45.4 %shard_map.86 = (bf16[256,256]{1,0:T(8,128)(2,1)}, f32[3,64,256]{2,1,0:T(8,128)}) custom-call(s32[1]{0:T(128)S(6)} %copy.11.start_ref, s32[1,1]{1,0:T(1,128)S(6)} %copy.12.len_ref, bf16[256,256]{1,0:T(8,128)(2,1)} %bitcast.6, bf16[256,256]{1,0:T(8,128)(2,1)} %bitcast.7, f32[1,256]{1,0:T(1,128)} %rate_ref.1, bf16[256,256]{1,0:T(8,128)(2,1)} %bitcast.8, ...), custom_call_target="tpu_custom_call" | custom-call | tf_op jit(solution)/shard_map/pallas_call | solution.py:235
  47.4 0.0 copy-start
  47.4 1.6 %copy.13 = bf16[1,256,256]{2,1,0:T(8,128)(2,1)} copy(bf16[1,256,256]{2,1,0:T(8,128)(2,1)} %bitcast.9) | data formatting | bytes 262144
  49.0 0.0 copy-done
  49.0 0.7 %copy.14 = f32[1,3,64,256]{3,2,1,0:T(8,128)} copy(f32[1,3,64,256]{3,2,1,0:T(8,128)S(1)} %bitcast.5) | data formatting | bytes 393216
Async XLA Ops:
  47.4 1.6 %copy-start = (f32[3,64,256]{2,1,0:T(8,128)S(1)}, f32[3,64,256]{2,1,0:T(8,128)}, u32[]{:S(2)}) copy-start(f32[3,64,256]{2,1,0:T(8,128)} %get-tuple-element.5) | copy-start | bytes 589828

commit v4 on v3

--- a/solution.py
+++ b/solution.py
@@ -146,7 +146,7 @@
                 for j in range(chunks):
                     up(z, r, j).start()
 
-        d = z + 1 + p - (z == 0).astype(jnp.int32)
+        d = z + p
 
         @pl.when((d < n) & (d > z))
         def _():
@@ -167,12 +167,13 @@
         for j in range(chunks):
             pl.when(z < n - 1)(lambda: up(z, 0, j).start())
             pl.when(z > 0)(lambda: down(z, 0, j).start())
-        pl.when(z > 0)(lambda: relay_up(0, 0, 1))
+        pl.when(z == 1)(lambda: relay_up(0, 0, 1))
         for r in range(1, m):
             for j in range(chunks):
                 give(r, j).wait_recv()
                 pl.when(z == 0)(lambda: up(z, r, j).start())
                 pl.when(z > 0)(lambda: down(z, r, j).start())
+        pl.when(z > 1)(lambda: relay_up(0, 0, 1))
         phase(0, 1)
         for r in range(1, m):
             give_q(r).wait_recv()

time: 49.8 us -> 44.7 us (0.90); the launches traced: 49.6 us -> 43.8 us
  Pallas kernels: 45.4 us -> 39.6 us
    pallas_call x1, Pallas kernels: 45.4 us -> 39.6 us  [per_device(): pl.pallas_call(functools.partial(kernel, n, m), out_shape=(jax.ShapeDtype...]
where the time goes in v4:
time: 44.7 us; the launch traced here: 43.8 us
  Pallas kernels  39.6 us (89%)
  local copies, waits for them, and re-layouts  2.29 us (5%)
  between operations  1.94 us (4%)
    pallas_call x1, Pallas kernels, per_device(): pl.pallas_call(functools.partial(kernel, n, m), out_shape=(jax.ShapeDtype...  39.6 us
    unnamed x4, local copies, waits for them, and re-layouts  2.29 us

profile of v4, /device:TPU:26, one launch (start us, length us, event | category | flops | bytes accessed | tf_op | source)
XLA Modules:
  0.0 43.8 jit_solution(4673369396635235986)
XLA Ops:
  1.9 39.6 %shard_map.86 = (bf16[256,256]{1,0:T(8,128)(2,1)}, f32[3,64,256]{2,1,0:T(8,128)}) custom-call(s32[1]{0:T(128)S(6)} %copy.11.start_ref, s32[1,1]{1,0:T(1,128)S(6)} %copy.12.len_ref, bf16[256,256]{1,0:T(8,128)(2,1)} %bitcast.6, bf16[256,256]{1,0:T(8,128)(2,1)} %bitcast.7, f32[1,256]{1,0:T(1,128)} %rate_ref.1, bf16[256,256]{1,0:T(8,128)(2,1)} %bitcast.8, ...), custom_call_target="tpu_custom_call" | custom-call | tf_op jit(solution)/shard_map/pallas_call | solution.py:236
  41.5 0.0 copy-start
  41.6 1.6 %copy.13 = bf16[1,256,256]{2,1,0:T(8,128)(2,1)} copy(bf16[1,256,256]{2,1,0:T(8,128)(2,1)} %bitcast.9) | data formatting | bytes 262144
  43.2 0.0 copy-done
  43.2 0.7 %copy.14 = f32[1,3,64,256]{3,2,1,0:T(8,128)} copy(f32[1,3,64,256]{3,2,1,0:T(8,128)S(1)} %bitcast.5) | data formatting | bytes 393216
Async XLA Ops:
  41.5 1.6 %copy-start = (f32[3,64,256]{2,1,0:T(8,128)S(1)}, f32[3,64,256]{2,1,0:T(8,128)}, u32[]{:S(2)}) copy-start(f32[3,64,256]{2,1,0:T(8,128)} %get-tuple-element.5) | copy-start | bytes 589828

commit v5 on v4

--- a/solution.py
+++ b/solution.py
@@ -198,7 +198,6 @@
                 for r in range(1, m):
                     give_out(r).start()
 
-            phase(c + 1, 0)
             xs = newton([grad[i] for i in range(3)])
             for i in range(3):
                 moved = state[i] - step_size * xs[i].astype(BF16).astype(F32)
@@ -206,6 +205,7 @@
                 ratio = (norm[i] + column_eps) / (after + column_eps)
                 state[i] = moved * jnp.sqrt(ratio)
                 norm[i] = after * ratio
+            phase(c + 1, 0)
 
         final_ref[...] = state[:, mine, :]
         for i in range(3):

time: 44.7 us -> 44.1 us (0.987); the launches traced: 43.8 us -> 43.9 us
  no operation moved by 1% of the time
where the time goes in v5:
time: 44.1 us; the launch traced here: 43.9 us
  Pallas kernels  39.7 us (90%)
  local copies, waits for them, and re-layouts  2.29 us (5%)
  between operations  1.94 us (4%)
    pallas_call x1, Pallas kernels, per_device(): pl.pallas_call(functools.partial(kernel, n, m), out_shape=(jax.ShapeDtype...  39.7 us
    unnamed x4, local copies, waits for them, and re-layouts  2.29 us

profile of v5, /device:TPU:26, one launch (start us, length us, event | category | flops | bytes accessed | tf_op | source)
XLA Modules:
  0.0 43.9 jit_solution(13417254209868872361)
XLA Ops:
  1.9 39.7 %shard_map.86 = (bf16[256,256]{1,0:T(8,128)(2,1)}, f32[3,64,256]{2,1,0:T(8,128)}) custom-call(s32[1]{0:T(128)S(6)} %copy.11.start_ref, s32[1,1]{1,0:T(1,128)S(6)} %copy.12.len_ref, bf16[256,256]{1,0:T(8,128)(2,1)} %bitcast.6, bf16[256,256]{1,0:T(8,128)(2,1)} %bitcast.7, f32[1,256]{1,0:T(1,128)} %rate_ref.1, bf16[256,256]{1,0:T(8,128)(2,1)} %bitcast.8, ...), custom_call_target="tpu_custom_call" | custom-call | tf_op jit(solution)/shard_map/pallas_call | solution.py:236
  41.6 0.0 copy-start
  41.6 1.6 %copy.13 = bf16[1,256,256]{2,1,0:T(8,128)(2,1)} copy(bf16[1,256,256]{2,1,0:T(8,128)(2,1)} %bitcast.9) | data formatting | bytes 262144
  43.2 0.0 copy-done
  43.2 0.7 %copy.14 = f32[1,3,64,256]{3,2,1,0:T(8,128)} copy(f32[1,3,64,256]{3,2,1,0:T(8,128)S(1)} %bitcast.5) | data formatting | bytes 393216
Async XLA Ops:
  41.6 1.6 %copy-start = (f32[3,64,256]{2,1,0:T(8,128)S(1)}, f32[3,64,256]{2,1,0:T(8,128)}, u32[]{:S(2)}) copy-start(f32[3,64,256]{2,1,0:T(8,128)} %get-tuple-element.5) | copy-start | bytes 589828
